TPU v7x, 512 devices: a whole 4x4x16 slice. The times are simulated.
512 devices in a mesh: region: 16 (over z), slab: 32 (over x, y, core).
Axes of the slice: x: 4, y: 4, z: 16, core: 2. Of those that a mesh axis runs over, the one named last changes fastest.
Arguments:
- records: bfloat16 [16384, 4096], P('region', 'slab'), may hold values from -6 to 6
- first_station: int32 [65536], P(('region', 'slab')), may hold values from 0 to 1023
- second_region: int32 [65536, 1], P(('region', 'slab')), may hold values from 0 to 15; in each aligned block of 128 rows (0 to 127, 128 to 255, ...) at most 16 rows name the same one
- second_station: int32 [65536], P(('region', 'slab')), may hold values from 0 to 1023
Outputs:
- stacks: bfloat16 [65536, 2048], P(('region', 'slab'))
Inputs may be any that keep to these rules, and one draw needn't show every extreme that they name: `second_region`: no region is named by more than 16 pairs of one device.
All inputs are finite; a program needn't handle non-finite values.
Results may differ from a plain program's by a relative error of at most 0.0077.
Values may be sent and summed in bfloat16 or wider, within the bound.
A program may use at most 64 MiB of HBM per device.

v0:
```python
import math
import jax
import jax.numpy as jnp
from jax import lax
from jax.sharding import PartitionSpec as P

NFFT = 2048
BINS = 1024
SEG = 2
HALF = 4


def dft_table():
    sample = jnp.arange(NFFT, dtype=jnp.int32)[:, None]
    frequency = jnp.arange(BINS, dtype=jnp.int32)[None, :]
    phase = (sample * frequency % NFFT).astype(jnp.float32) * (2.0 * math.pi / NFFT)
    return jnp.concatenate([jnp.cos(phase), -jnp.sin(phase)], axis=1).astype(jnp.bfloat16)


def whitened(traces):
    count = traces.shape[0]
    signal = traces.astype(jnp.float32).reshape(count * SEG, NFFT)
    signal = signal - jnp.mean(signal, axis=1, keepdims=True)
    position = jnp.arange(NFFT, dtype=jnp.int32).astype(jnp.float32)
    taper = 0.5 - 0.5 * jnp.cos(position * (2.0 * math.pi / NFFT))
    tapered = (signal * taper[None, :]).astype(jnp.bfloat16)
    spectrum = jnp.dot(tapered, dft_table(), preferred_element_type=jnp.float32)
    real_part = spectrum[:, :BINS]
    imag_part = spectrum[:, BINS:]
    amplitude = jnp.sqrt(real_part * real_part + imag_part * imag_part + 1e-06)
    padded = jnp.pad(amplitude, ((0, 0), (HALF, HALF)))
    smooth = jnp.zeros_like(amplitude)
    for offset in range(2 * HALF + 1):
        smooth = smooth + padded[:, offset : offset + BINS]
    smooth = smooth / (2 * HALF + 1)
    level = jnp.mean(amplitude, axis=1, keepdims=True)
    divisor = smooth + level + 1e-06
    white = spectrum / jnp.concatenate([divisor, divisor], axis=1)
    return white.astype(jnp.bfloat16).reshape(count, SEG * NFFT)


def cross(first_rows, second_rows):
    left = first_rows.astype(jnp.float32).reshape(first_rows.shape[:-1] + (SEG, 2, BINS))
    right = second_rows.astype(jnp.float32).reshape(second_rows.shape[:-1] + (SEG, 2, BINS))
    real_sum = jnp.mean(
        left[..., 0, :] * right[..., 0, :] + left[..., 1, :] * right[..., 1, :], axis=-2
    )
    imag_sum = jnp.mean(
        left[..., 0, :] * right[..., 1, :] - left[..., 1, :] * right[..., 0, :], axis=-2
    )
    return jnp.concatenate([real_sum, imag_sum], axis=-1).astype(jnp.bfloat16)


def local(records, first_station, second_region, second_station):
    regions = lax.axis_size("region")
    pair_count = first_station.shape[0]
    capacity = max(2, pair_count // regions + pair_count // 16)
    arrived = lax.all_to_all(records, "slab", split_axis=0, concat_axis=1, tiled=True)
    spectra = whitened(arrived)
    width = spectra.shape[1]
    target = second_region[:, 0]
    onehot = (target[:, None] == jnp.arange(regions, dtype=jnp.int32)[None, :]).astype(jnp.int32)
    ranking = jnp.sum((jnp.cumsum(onehot, axis=0) - onehot) * onehot, axis=1)
    slot_index = target * capacity + ranking
    requests = (
        jnp.zeros((regions * capacity,), jnp.int32)
        .at[slot_index]
        .set(second_station)
        .reshape(regions, capacity)
    )
    incoming = lax.all_to_all(requests, "region", split_axis=0, concat_axis=0, tiled=True)
    wanted = jnp.concatenate([first_station, incoming.reshape(-1)])
    initial = jnp.zeros((wanted.shape[0], width), jnp.bfloat16)
    piece = lax.all_gather(spectra, "slab", axis=0, tiled=True)
    inside = (wanted >= 0) & (wanted < piece.shape[0])
    chosen = jnp.take(piece, jnp.clip(wanted, 0, piece.shape[0] - 1), axis=0)
    picked = jnp.where(inside[:, None], chosen, initial)
    first_rows = picked[:pair_count]
    served = picked[pair_count:]
    returned = lax.all_to_all(
        served.reshape(regions, capacity, width), "region", split_axis=0, concat_axis=0, tiled=True
    )
    second_rows = jnp.take(returned.reshape(regions * capacity, width), slot_index, axis=0)
    stacks = cross(first_rows, second_rows)
    return stacks


def solution(mesh):
    placed = (
        P("region", "slab"),
        P(("region", "slab")),
        P(("region", "slab"), None),
        P(("region", "slab")),
    )
    return jax.shard_map(
        local, mesh=mesh, in_specs=placed, out_specs=P(("region", "slab"), None), check_vma=False
    )
```

profile of v0, /device:TPU:32, one launch (start us, length us, event | category | flops | bytes accessed | tf_op | source)
XLA Modules:
  0.0 269.8 jit_solution(3383094113395302440)
XLA Ops:
  6.5 7.3 %all-to-all-start.1 = ((bf16[32,32,128]{2,1,0:T(8,128)(2,1)}), bf16[32,32,128]{2,1,0:T(8,128)(2,1)S(1)}, u32[]{:S(2)}, u32[]{:S(2)}) async-start(bf16[32,32,128]{2,1,0:T(8,128)(2,1)} %bitcast.20), calls=%async_computation.1 | async-start | bytes 524288 | tf_op jit(solution)/shard_map/all_to_all | solution.py:58
  13.9 0.0 all-gather.2.cloned.1.call-start
  13.9 34.9 %negate_convert_fusion = (bf16[2048,1024]{1,0:T(8,128)(2,1)}, bf16[2048,1024]{1,0:T(8,128)(2,1)}) fusion(), kind=kLoop, calls=%fused_computation.13 | loop fusion | flops 35651584 | bytes 8388608 | tf_op jit(solution)/shard_map/convert.6
  48.9 0.1 multiply_subtract_fusion
  48.9 0.0 all-to-all-done.1
  48.9 0.2 convert_reduce_fusion
  49.1 0.1 copy.8
  49.2 0.1 reduce_sum.60
  49.3 0.1 reduce_sum.61
  49.4 0.1 convert_bitcast_fusion
  49.5 0.3 copy.7
  49.8 0.1 reshape.149
  49.9 0.0 copy-start.2
  49.9 0.0 copy-start.3
  49.9 4.4 %fusion.3 = f32[64,2048]{1,0:T(8,128)S(1)} fusion(bf16[2048,1024]{1,0:T(8,128)(2,1)} %get-tuple-element.13, bf16[2048,1024]{1,0:T(8,128)(2,1)} %get-tuple-element.14, f32[64,2048]{1,0:T(8,128)S(1)} %reshape.149, f32[2048]{0:T(1024)S(1)} %multiply_subtract_fusion, f32[64]{0:T(128)S(1)} %broadcast_multiply_fusion.1), kind=kOutput, calls=%fused_computation.9 | convolution fusion | flops 554041344 | bytes 9445632 | tf_op jit(solution)/shard_map/dot_general | solution.py:27
  54.3 0.2 fusion.33
  54.5 0.6 fusion.22
  55.2 0.1 fusion.11
  55.2 0.8 reshape.144
  56.0 0.0 all-gather.2.cloned.1.call-update
  56.0 0.0 copy-done.2
  56.0 0.1 fusion.28
  56.1 0.2 reduce_window_sum.11
  56.3 0.2 select_reduce_fusion
  56.5 1.1 scatter_custom_fusion
  57.6 0.7 all_to_all.19
  58.3 15.2 %all-to-all-start = ((s32[16,1,16]{2,1,0:T(1,128)}), s32[16,1,16]{2,1,0:T(1,128)S(1)}, u32[]{:S(2)}, u32[]{:S(2)}) async-start(s32[16,1,16]{2,1,0:T(1,128)} %all_to_all.19), calls=%async_computation | async-start | bytes 16384 | tf_op jit(solution)/shard_map/all_to_all | solution.py:71
  73.5 0.0 copy-done.3
  73.5 11.0 %all-to-all-done = s32[16,1,16]{2,1,0:T(1,128)S(1)} async-done(((s32[16,1,16]{2,1,0:T(1,128)}), s32[16,1,16]{2,1,0:T(1,128)S(1)}, u32[]{:S(2)}, u32[]{:S(2)}) %all-to-all-start) | async-done | bytes 1056 | tf_op jit(solution)/shard_map/all_to_all | solution.py:71
  84.6 0.1 concatenate.43
  84.6 0.5 broadcast.142
  85.1 0.6 reduce.12
  85.7 0.1 concatenate.38
  85.9 42.7 %all-gather.2.cloned.1.call-done = bf16[1024,4096]{1,0:T(8,128)(2,1)} async-done(((bf16[32,4096]{1,0:T(8,128)(2,1)}), bf16[1024,4096]{1,0:T(8,128)(2,1)}) %all-gather.2.cloned.1.call-update) | async-done | bytes 8388624 | tf_op jit(solution)/shard_map/all_gather | solution.py:74
  128.6 12.0 %gather_fusion = bf16[384,4096]{1,0:T(8,128)(2,1)S(1)} fusion(bf16[1024,4096]{1,0:T(8,128)(2,1)} %all-gather.2.cloned.1.call-done, s32[1024]{0:T(1024)S(1)} %pad_clamp_fusion.1), kind=kCustom, calls=%fused_computation | custom fusion | bytes 6292992 | tf_op jit(solution)/shard_map/jit(_take)/gather | solution.py:76
  140.5 0.5 select_select_fusion
  141.0 0.0 copy-start
  141.0 1.7 copy-done
  142.7 1.5 slice.77
  144.2 12.7 %all-to-all-start.2 = ((bf16[16,16,4096]{2,1,0:T(8,128)(2,1)}), bf16[16,16,4096]{2,1,0:T(8,128)(2,1)S(1)}, u32[]{:S(2)}, u32[]{:S(2)}) async-start(bf16[16,16,4096]{2,1,0:T(8,128)(2,1)} %bitcast.19), calls=%async_computation.2 | async-start | bytes 4194304 | tf_op jit(solution)/shard_map/all_to_all | solution.py:80
  156.9 2.8 %slice_convert_fusion = f32[128,4096]{1,0:T(8,128)} fusion(bf16[384,4096]{1,0:T(8,128)(2,1)} %copy-done), kind=kLoop, calls=%fused_computation.21 | loop fusion | flops 524288 | bytes 3145728 | tf_op jit(solution)/shard_map/reshape | solution.py:43
  159.7 4.0 %reshape.151 = f32[128,2,2,1024]{3,2,1,0:T(2,128)} reshape(f32[128,4096]{1,0:T(8,128)} %slice_convert_fusion) | data formatting | bytes 4194304 | tf_op jit(solution)/shard_map/reshape | solution.py:43
  163.7 87.5 %all-to-all-done.2 = bf16[16,16,4096]{2,1,0:T(8,128)(2,1)S(1)} async-done(((bf16[16,16,4096]{2,1,0:T(8,128)(2,1)}), bf16[16,16,4096]{2,1,0:T(8,128)(2,1)S(1)}, u32[]{:S(2)}, u32[]{:S(2)}) %all-to-all-start.2) | async-done | bytes 2097184 | tf_op jit(solution)/shard_map/all_to_all | solution.py:80
  251.2 1.2 gather_fusion.1
  252.4 0.0 copy-start.1
  252.4 1.6 gather.12
  254.0 2.2 fusion.10
  256.2 0.0 copy-done.1
  256.2 5.8 %add_reduce_fusion = (f32[128,1024]{1,0:T(8,128)S(1)}, f32[128,1024]{1,0:T(8,128)S(1)}) fusion(f32[128,2,2,1024]{3,2,1,0:T(2,128)S(1)} %fusion.10, f32[128,2,2,1024]{3,2,1,0:T(2,128)S(1)} %copy-done.1), kind=kLoop, calls=%fused_computation.23 | loop fusion | flops 1835008 | bytes 5242880 | tf_op jit(solution)/shard_map/reduce_sum | solution.py:45
  262.1 0.8 pad_maximum_fusion
  (12 shorter events, 0.2 us)
Async XLA Ops:
  6.5 42.4 %all-to-all-start.1 = ((bf16[32,32,128]{2,1,0:T(8,128)(2,1)}), bf16[32,32,128]{2,1,0:T(8,128)(2,1)S(1)}, u32[]{:S(2)}, u32[]{:S(2)}) async-start(bf16[32,32,128]{2,1,0:T(8,128)(2,1)} %bitcast.20), calls=%async_computation.1 | async-start | bytes 524288 | tf_op jit(solution)/shard_map/all_to_all | solution.py:58
  13.9 114.7 %all-gather.2.cloned.1.call-start = ((), (), s32[]{:S(2)}) async-start(), calls=%async_computation.3 | async-start | bytes 8650752 | tf_op jit(solution)/shard_map/all_gather | solution.py:74
  49.9 6.2 %copy-start.2 = (s32[128,1]{0,1:T(1,128)S(1)}, s32[128,1]{0,1:T(1,128)}, u32[]{:S(2)}) copy-start(s32[128,1]{0,1:T(1,128)} %param.6) | copy-start | bytes 1540
  49.9 23.6 %copy-start.3 = (s32[128]{0:T(128)S(1)}, s32[128]{0:T(128)}, u32[]{:S(2)}) copy-start(s32[128]{0:T(128)} %param.5) | copy-start | bytes 1540
  58.3 26.3 %all-to-all-start = ((s32[16,1,16]{2,1,0:T(1,128)}), s32[16,1,16]{2,1,0:T(1,128)S(1)}, u32[]{:S(2)}, u32[]{:S(2)}) async-start(s32[16,1,16]{2,1,0:T(1,128)} %all_to_all.19), calls=%async_computation | async-start | bytes 16384 | tf_op jit(solution)/shard_map/all_to_all | solution.py:71
  141.0 1.7 copy-start
  144.2 107.0 %all-to-all-start.2 = ((bf16[16,16,4096]{2,1,0:T(8,128)(2,1)}), bf16[16,16,4096]{2,1,0:T(8,128)(2,1)S(1)}, u32[]{:S(2)}, u32[]{:S(2)}) async-start(bf16[16,16,4096]{2,1,0:T(8,128)(2,1)} %bitcast.19), calls=%async_computation.2 | async-start | bytes 4194304 | tf_op jit(solution)/shard_map/all_to_all | solution.py:80
  252.4 3.8 %copy-start.1 = (f32[128,2,2,1024]{3,2,1,0:T(2,128)S(1)}, f32[128,2,2,1024]{3,2,1,0:T(2,128)}, u32[]{:S(2)}) copy-start(f32[128,2,2,1024]{3,2,1,0:T(2,128)} %reshape.151) | copy-start | bytes 6291460
Sparse Core Ops, SparseCore 0:
  56.2 72.3 all-gather.1
where the time goes:
time: 270 us
  waiting for transfers between devices  141 us (52%)
  other arithmetic  49.5 us (18%)
  starting transfers between devices  35.2 us (13%)
  local copies, waits for them, and re-layouts  25.8 us (10%)
  between operations  13.6 us (5%)
  matrix products  4.41 us (2%)
    all_to_all x1, waiting for transfers between devices, local(): lax.all_to_all(served.reshape(regions, capacity, width), 'region', split_...  87.5 us
    all_gather x1, waiting for transfers between devices, local(): piece = lax.all_gather(spectra, 'slab', axis=0, tiled=True)  42.7 us
    another operation x3, other arithmetic  35 us
    all_to_all x1, starting transfers between devices, local(): lax.all_to_all(requests, 'region', split_axis=0, concat_axis=0, tiled=True)  15.2 us
    all_to_all x1, starting transfers between devices, local(): lax.all_to_all(served.reshape(regions, capacity, width), 'region', split_...  12.7 us
    gather x1, local copies, waits for them, and re-layouts, local(): chosen = jnp.take(piece, jnp.clip(wanted, 0, piece.shape[0] - 1), axis=0)  12 us
    all_to_all x1, waiting for transfers between devices, local(): lax.all_to_all(requests, 'region', split_axis=0, concat_axis=0, tiled=True)  11 us
    all_to_all x1, starting transfers between devices, local(): lax.all_to_all(records, 'slab', split_axis=0, concat_axis=1, tiled=True)  7.32 us
  transfers between devices with their start and end apart: 4, of which 3 were waited for; matrix products, arithmetic and copies ran while one was open for 17% of the time, Pallas kernels for 0%

commit v1 on v0

--- a/solution.py
+++ b/solution.py
@@ -71,7 +71,9 @@
     incoming = lax.all_to_all(requests, "region", split_axis=0, concat_axis=0, tiled=True)
     wanted = jnp.concatenate([first_station, incoming.reshape(-1)])
     initial = jnp.zeros((wanted.shape[0], width), jnp.bfloat16)
-    piece = lax.all_gather(spectra, "slab", axis=0, tiled=True)
+    piece = jnp.concatenate(
+        lax.all_to_all(jnp.stack([spectra] * lax.axis_size("slab")), "slab", 0, 0), axis=0
+    )
     inside = (wanted >= 0) & (wanted < piece.shape[0])
     chosen = jnp.take(piece, jnp.clip(wanted, 0, piece.shape[0] - 1), axis=0)
     picked = jnp.where(inside[:, None], chosen, initial)

time: 270 us -> 338 us (1.25)
  the two profiles are of different devices: /device:TPU:32 before, /device:TPU:8 now
where the time goes in v1:
time: 338 us
  waiting for transfers between devices  218 us (64%)
  other arithmetic  49.6 us (15%)
  starting transfers between devices  36.4 us (11%)
  local copies, waits for them, and re-layouts  29.4 us (9%)
  matrix products  4.41 us (1%)
    all_to_all x1, waiting for transfers between devices, local(): lax.all_to_all(jnp.stack([spectra] * lax.axis_size('slab')), 'slab', 0, 0)  123 us
    all_to_all x1, waiting for transfers between devices, local(): lax.all_to_all(served.reshape(regions, capacity, width), 'region', split_...  88.8 us
    another operation x3, other arithmetic  35 us
    all_to_all x1, starting transfers between devices, local(): lax.all_to_all(requests, 'region', split_axis=0, concat_axis=0, tiled=True)  13.4 us
    gather x1, local copies, waits for them, and re-layouts, local(): chosen = jnp.take(piece, jnp.clip(wanted, 0, piece.shape[0] - 1), axis=0)  12 us
    all_to_all x1, starting transfers between devices, local(): lax.all_to_all(records, 'slab', split_axis=0, concat_axis=1, tiled=True)  9.35 us
    all_to_all x1, starting transfers between devices, local(): lax.all_to_all(jnp.stack([spectra] * lax.axis_size('slab')), 'slab', 0, 0)  7.57 us
  transfers between devices with their start and end apart: 4, of which 3 were waited for; matrix products, arithmetic and copies ran while one was open for 15% of the time, Pallas kernels for 0%

profile of v1, /device:TPU:8, one launch (start us, length us, event | category | flops | bytes accessed | tf_op | source)
XLA Modules:
  0.0 337.5 jit_solution(3331669043079729801)
XLA Ops:
  0.0 9.4 %all-to-all-start.1 = ((bf16[32,32,128]{2,1,0:T(8,128)(2,1)}), bf16[32,32,128]{2,1,0:T(8,128)(2,1)S(1)}, u32[]{:S(2)}, u32[]{:S(2)}) async-start(bf16[32,32,128]{2,1,0:T(8,128)(2,1)} %bitcast.20), calls=%async_computation.1 | async-start | bytes 524288 | tf_op jit(solution)/shard_map/all_to_all | solution.py:58
  9.4 0.0 copy-start.2
  9.4 34.9 %negate_convert_fusion = (bf16[2048,1024]{1,0:T(8,128)(2,1)}, bf16[2048,1024]{1,0:T(8,128)(2,1)}) fusion(), kind=kLoop, calls=%fused_computation.13 | loop fusion | flops 35651584 | bytes 8388608 | tf_op jit(solution)/shard_map/convert.6
  44.3 0.0 copy-done.2
  44.3 0.1 fusion.28
  44.4 0.2 reduce_window_sum.11
  44.6 0.2 select_reduce_fusion
  44.8 1.1 scatter_custom_fusion
  45.9 0.7 all_to_all.22
  46.6 0.1 multiply_subtract_fusion
  46.6 0.0 all-to-all-done.1
  46.6 13.4 %all-to-all-start = ((s32[16,1,16]{2,1,0:T(1,128)}), s32[16,1,16]{2,1,0:T(1,128)S(1)}, u32[]{:S(2)}, u32[]{:S(2)}) async-start(s32[16,1,16]{2,1,0:T(1,128)} %all_to_all.22), calls=%async_computation | async-start | bytes 16384 | tf_op jit(solution)/shard_map/all_to_all | solution.py:71
  60.0 0.1 convert_bitcast_fusion
  60.1 0.3 copy.7
  60.4 0.1 reshape.151
  60.5 0.2 convert_reduce_fusion
  60.7 0.1 copy.8
  60.8 0.1 reduce_sum.60
  60.9 0.1 reduce_sum.61
  61.0 4.4 %fusion.3 = f32[64,2048]{1,0:T(8,128)S(1)} fusion(bf16[2048,1024]{1,0:T(8,128)(2,1)} %get-tuple-element.13, bf16[2048,1024]{1,0:T(8,128)(2,1)} %get-tuple-element.14, f32[64,2048]{1,0:T(8,128)S(1)} %reshape.151, f32[2048]{0:T(1024)S(1)} %multiply_subtract_fusion, f32[64]{0:T(128)S(1)} %broadcast_multiply_fusion.1), kind=kOutput, calls=%fused_computation.9 | convolution fusion | flops 554041344 | bytes 9445632 | tf_op jit(solution)/shard_map/dot_general | solution.py:27
  65.4 0.2 fusion.33
  65.6 0.6 fusion.22
  66.2 0.1 fusion.11
  66.3 0.1 stack_reshape.2
  66.4 6.0 %all-to-all-done = s32[16,1,16]{2,1,0:T(1,128)S(1)} async-done(((s32[16,1,16]{2,1,0:T(1,128)}), s32[16,1,16]{2,1,0:T(1,128)S(1)}, u32[]{:S(2)}, u32[]{:S(2)}) %all-to-all-start) | async-done | bytes 1056 | tf_op jit(solution)/shard_map/all_to_all | solution.py:71
  72.4 4.3 %stack.3 = bf16[32,32,4096]{2,1,0:T(8,128)(2,1)} broadcast(bf16[32,4096]{1,0:T(8,128)(2,1)S(1)} %stack_reshape.2), dimensions={1,2} | broadcast | bytes 8650752 | tf_op jit(solution)/shard_map/stack | solution.py:75
  76.7 0.0 copy-start.3
  76.7 7.6 %all-to-all-start.2 = ((bf16[32,32,4096]{2,1,0:T(8,128)(2,1)}), bf16[32,32,4096]{2,1,0:T(8,128)(2,1)}, u32[]{:S(2)}, u32[]{:S(2)}) async-start(bf16[32,32,4096]{2,1,0:T(8,128)(2,1)} %stack.3), calls=%async_computation.2 | async-start | bytes 16777216 | tf_op jit(solution)/shard_map/all_to_all | solution.py:75
  84.2 0.0 copy-done.3
  84.3 0.1 concatenate.43
  84.4 0.5 broadcast.143
  84.9 0.7 reduce.12
  85.5 0.1 concatenate.38
  85.7 122.8 %all-to-all-done.2 = bf16[32,32,4096]{2,1,0:T(8,128)(2,1)} async-done(((bf16[32,32,4096]{2,1,0:T(8,128)(2,1)}), bf16[32,32,4096]{2,1,0:T(8,128)(2,1)}, u32[]{:S(2)}, u32[]{:S(2)}) %all-to-all-start.2) | async-done | bytes 8388640 | tf_op jit(solution)/shard_map/all_to_all | solution.py:75
  208.5 12.0 %gather_fusion = bf16[384,4096]{1,0:T(8,128)(2,1)S(1)} fusion(bf16[1024,4096]{1,0:T(8,128)(2,1)} %bitcast.6, s32[1024]{0:T(1024)S(1)} %pad_clamp_fusion.1), kind=kCustom, calls=%fused_computation | custom fusion | bytes 6292992 | tf_op jit(solution)/shard_map/jit(_take)/gather | solution.py:78
  220.5 0.5 select_select_fusion
  220.9 0.0 copy-start
  221.0 1.7 copy-done
  222.6 1.5 slice.77
  224.1 6.0 %all-to-all-start.3 = ((bf16[16,16,4096]{2,1,0:T(8,128)(2,1)}), bf16[16,16,4096]{2,1,0:T(8,128)(2,1)S(1)}, u32[]{:S(2)}, u32[]{:S(2)}) async-start(bf16[16,16,4096]{2,1,0:T(8,128)(2,1)} %bitcast.19), calls=%async_computation.3 | async-start | bytes 4194304 | tf_op jit(solution)/shard_map/all_to_all | solution.py:82
  230.2 2.8 slice_convert_fusion
  233.0 4.0 %reshape.153 = f32[128,2,2,1024]{3,2,1,0:T(2,128)} reshape(f32[128,4096]{1,0:T(8,128)} %slice_convert_fusion) | data formatting | bytes 4194304 | tf_op jit(solution)/shard_map/reshape | solution.py:43
  237.0 88.8 %all-to-all-done.3 = bf16[16,16,4096]{2,1,0:T(8,128)(2,1)S(1)} async-done(((bf16[16,16,4096]{2,1,0:T(8,128)(2,1)}), bf16[16,16,4096]{2,1,0:T(8,128)(2,1)S(1)}, u32[]{:S(2)}, u32[]{:S(2)}) %all-to-all-start.3) | async-done | bytes 2097184 | tf_op jit(solution)/shard_map/all_to_all | solution.py:82
  325.8 1.2 gather_fusion.1
  327.0 0.0 copy-start.1
  327.0 1.6 gather.12
  328.6 2.2 fusion.10
  330.8 0.0 copy-done.1
  330.9 5.8 %add_reduce_fusion = (f32[128,1024]{1,0:T(8,128)S(1)}, f32[128,1024]{1,0:T(8,128)S(1)}) fusion(f32[128,2,2,1024]{3,2,1,0:T(2,128)S(1)} %fusion.10, f32[128,2,2,1024]{3,2,1,0:T(2,128)S(1)} %copy-done.1), kind=kLoop, calls=%fused_computation.23 | loop fusion | flops 1835008 | bytes 5242880 | tf_op jit(solution)/shard_map/reduce_sum | solution.py:45
  336.7 0.8 pad_maximum_fusion
  (12 shorter events, 0.2 us)
Async XLA Ops:
  0.0 46.6 %all-to-all-start.1 = ((bf16[32,32,128]{2,1,0:T(8,128)(2,1)}), bf16[32,32,128]{2,1,0:T(8,128)(2,1)S(1)}, u32[]{:S(2)}, u32[]{:S(2)}) async-start(bf16[32,32,128]{2,1,0:T(8,128)(2,1)} %bitcast.20), calls=%async_computation.1 | async-start | bytes 524288 | tf_op jit(solution)/shard_map/all_to_all | solution.py:58
  9.4 35.0 %copy-start.2 = (s32[128,1]{0,1:T(1,128)S(1)}, s32[128,1]{0,1:T(1,128)}, u32[]{:S(2)}) copy-start(s32[128,1]{0,1:T(1,128)} %param.6) | copy-start | bytes 1540
  46.6 25.8 %all-to-all-start = ((s32[16,1,16]{2,1,0:T(1,128)}), s32[16,1,16]{2,1,0:T(1,128)S(1)}, u32[]{:S(2)}, u32[]{:S(2)}) async-start(s32[16,1,16]{2,1,0:T(1,128)} %all_to_all.22), calls=%async_computation | async-start | bytes 16384 | tf_op jit(solution)/shard_map/all_to_all | solution.py:71
  76.7 7.6 %copy-start.3 = (s32[128]{0:T(128)S(1)}, s32[128]{0:T(128)}, u32[]{:S(2)}) copy-start(s32[128]{0:T(128)} %param.5) | copy-start | bytes 1540
  76.7 131.8 %all-to-all-start.2 = ((bf16[32,32,4096]{2,1,0:T(8,128)(2,1)}), bf16[32,32,4096]{2,1,0:T(8,128)(2,1)}, u32[]{:S(2)}, u32[]{:S(2)}) async-start(bf16[32,32,4096]{2,1,0:T(8,128)(2,1)} %stack.3), calls=%async_computation.2 | async-start | bytes 16777216 | tf_op jit(solution)/shard_map/all_to_all | solution.py:75
  220.9 1.7 copy-start
  224.1 101.7 %all-to-all-start.3 = ((bf16[16,16,4096]{2,1,0:T(8,128)(2,1)}), bf16[16,16,4096]{2,1,0:T(8,128)(2,1)S(1)}, u32[]{:S(2)}, u32[]{:S(2)}) async-start(bf16[16,16,4096]{2,1,0:T(8,128)(2,1)} %bitcast.19), calls=%async_computation.3 | async-start | bytes 4194304 | tf_op jit(solution)/shard_map/all_to_all | solution.py:82
  327.0 3.8 %copy-start.1 = (f32[128,2,2,1024]{3,2,1,0:T(2,128)S(1)}, f32[128,2,2,1024]{3,2,1,0:T(2,128)}, u32[]{:S(2)}) copy-start(f32[128,2,2,1024]{3,2,1,0:T(2,128)} %reshape.153) | copy-start | bytes 6291460
